TPU v7x, 32 devices: a whole 2x2x4 slice. The times are simulated.
32 devices in a mesh: gz: 2 (over core), row: 4 (over y, x), col: 4 (over z).
Axes of the slice: x: 2, y: 2, z: 4, core: 2. Of those that a mesh axis runs over, the one named last changes fastest.
Arguments:
- l_panel: float32 [2, 8, 4, 8, 128, 256], P('gz', None, 'row', 'col'), may hold values from -6 to 6
- l_rows: int32 [2, 8, 4, 8], P('gz', None, 'row'), may hold values from -1 to 7, as said below
- u_panel: float32 [2, 8, 4, 16, 256, 128], P('gz', None, 'col', 'row'), may hold values from -0.125 to 0.125
- u_cols: int32 [2, 8, 4, 16], P('gz', None, 'col'), may hold values from -1 to 15, as said below
- u11_inv: float32 [2, 8, 256, 256], P('gz'), as said below
- ancestor: float32 [4, 1024, 8192], P('row', 'gz', 'col'), may hold values from -6 to 6
Outputs:
- schur: float32 [4, 1024, 8192], P('row', 'gz', 'col')
Inputs may be any that keep to these rules, and one draw needn't show every extreme that they name: `l_rows`: within one layer, supernode and process row the live entries are distinct; at most 8 are live, and in every layer and process row some supernode has all 8 live. `u_cols`: within one layer, supernode and process column the live entries are distinct; at most 16 are live, and in every layer and process column some supernode has all 16 live. `u11_inv`: upper triangular, with diagonal entries between 0.5 and 1.5.
All inputs are finite; a program needn't handle non-finite values.
Results may differ from a plain program's by a relative error of at most 0.000058.
Values sent between devices are 32-bit elements; how exact they have to be, the bound alone decides.
No kernel may reach another device: no remote copies, remote signals or barrier semaphores. Data moves between devices by JAX's collectives and lax.ppermute only.
A program may use at most 128 MiB of HBM per device.

v0:
```python
import jax
import jax.numpy as jnp
from jax import lax
from jax.sharding import PartitionSpec as P

W = 256
B = 128
AR = 8
AC = 16
highest = lax.Precision.HIGHEST


def place_rows(targets, blocks):
    onehot = (targets[:, None, :] == jnp.arange(AR, dtype=jnp.int32)[None, :, None]).astype(
        jnp.float32
    )
    return jnp.einsum("sak,skbw->absw", onehot, blocks, precision=highest)


def place_columns(targets, blocks):
    onehot = (targets[:, None, :] == jnp.arange(AC, dtype=jnp.int32)[None, :, None]).astype(
        jnp.float32
    )
    return jnp.einsum("sak,skwb->swab", onehot, blocks, precision=highest)


def body(l_panel, l_rows, u_panel, u_cols, u11_inv, ancestor):
    l_blocks = l_panel[0, :, 0]
    scaled = jnp.einsum("skbw,swv->skbv", l_blocks, u11_inv[0], precision=highest)
    row_targets = l_rows[0, :, 0]
    col_targets = u_cols[0, :, 0]
    u_blocks = u_panel[0, :, 0]
    supernodes = scaled.shape[0]
    targets = row_targets
    l_placed = place_rows(targets, lax.all_gather(scaled, "col", axis=1, tiled=True))
    targets = col_targets
    u_placed = place_columns(targets, lax.all_gather(u_blocks, "row", axis=1, tiled=True))
    l_matrix = l_placed.reshape(AR * B, supernodes * W)
    u_matrix = u_placed.reshape(supernodes * W, AC * B)
    half_rows = ancestor.shape[1]
    summed = lax.psum(jnp.dot(l_matrix, u_matrix, precision=highest), "gz")
    own_share = lax.dynamic_slice_in_dim(summed, lax.axis_index("gz") * half_rows, half_rows, 0)
    return ancestor - own_share[None]


def solution(mesh):
    in_specs = (
        P("gz", None, "row", "col", None, None),
        P("gz", None, "row", None),
        P("gz", None, "col", "row", None, None),
        P("gz", None, "col", None),
        P("gz", None, None, None),
        P("row", "gz", "col"),
    )
    out_specs = P("row", "gz", "col")
    return jax.shard_map(body, mesh=mesh, in_specs=in_specs, out_specs=out_specs, check_vma=False)
```

profile of v0, /device:TPU:0, one launch (start us, length us, event | category | flops | bytes accessed | tf_op | source)
XLA Modules:
  0.0 466.4 jit_solution(12975585213557576710)
XLA Ops:
  6.5 0.0 copy-start
  6.5 0.0 all-gather.4.cloned.1.call-start
  6.5 1.6 copy-done
  8.1 5.1 %fusion.11 = f32[8,2,128,256]{3,2,0,1:T(8,128)} fusion(f32[1,8,256,256]{3,2,1,0:T(8,128)S(1)} %copy-done, f32[1,8,1,2,128,256]{5,4,3,2,1,0:T(8,128)} %param.6), kind=kOutput, calls=%fused_computation.10 | convolution fusion | flops 1610612736 | bytes 6291456 | tf_op jit(solution)/shard_map/skbw,swv->skbv/dot_general | solution.py:29
  13.2 0.0 all-gather.4.cloned.1.call-update
  13.2 0.0 all-gather.6.cloned.1.call-start
  13.3 4.7 copy.13
  17.9 0.0 all-gather.6.cloned.1.call-update
  17.9 0.0 all-reduce.2.cloned.1.call-start
  18.0 147.7 %all-gather.4.cloned.1.call-done = f32[8,8,128,256]{3,2,0,1:T(8,128)} async-done(((f32[8,2,128,256]{3,2,0,1:T(8,128)}), f32[8,8,128,256]{3,2,0,1:T(8,128)}) %all-gather.4.cloned.1.call-update) | async-done | bytes 8388624 | tf_op jit(solution)/shard_map/all_gather | solution.py:35
  165.7 0.0 copy-done.4
  165.7 12.5 %fusion.8 = f32[8,128,8,256]{3,0,1,2:T(8,128)S(1)} fusion(f32[8,8,128,256]{3,2,0,1:T(8,128)} %all-gather.4.cloned.1.call-done, s32[8,8]{1,0:T(8,128)S(1)} %bitcast.41), kind=kOutput, calls=%fused_computation.9 | convolution fusion | flops 201327104 | bytes 16777472 | tf_op jit(solution)/shard_map/sak,skbw->absw/dot_general | solution.py:17
  178.2 4.9 %copy.12 = f32[8,128,8,256]{3,2,1,0:T(8,128)S(1)} copy(f32[8,128,8,256]{3,0,1,2:T(8,128)S(1)} %fusion.8) | data formatting | bytes 16777216 | tf_op jit(solution)/shard_map/sak,skbw->absw/transpose | solution.py:17
  183.0 0.0 copy-start.3
  183.0 7.3 %copy.19 = f32[128,8,8,256]{3,1,2,0:T(8,128)} copy(f32[128,8,8,256]{3,2,1,0:T(8,128)S(1)} %bitcast.38) | data formatting | bytes 16777216
  190.4 132.9 %all-gather.6.cloned.1.call-done = f32[1,8,1,16,256,128]{5,4,2,1,0,3:T(8,128)} async-done(((f32[1,8,1,4,256,128]{5,4,2,1,0,3:T(8,128)}), f32[1,8,1,16,256,128]{5,4,2,1,0,3:T(8,128)}) %all-gather.6.cloned.1.call-update) | async-done | bytes 16777232 | tf_op jit(solution)/shard_map/all_gather | solution.py:37
  323.2 0.0 copy-done.3
  323.2 25.9 %fusion.3 = f32[8,16,256,128]{3,1,2,0:T(8,128)} fusion(f32[1,8,1,16,256,128]{5,4,2,1,0,3:T(8,128)} %all-gather.6.cloned.1.call-done, s32[8,16]{1,0:T(8,128)S(1)} %bitcast.40), kind=kOutput, calls=%fused_computation.3 | convolution fusion | flops 805308416 | bytes 33554944 | tf_op jit(solution)/shard_map/sak,skwb->swab/dot_general | solution.py:24
  349.1 0.0 copy-done.2
  349.1 64.9 %fusion = f32[1024,2048]{1,0:T(8,128)} fusion(f32[1024,2048]{1,0:T(8,128)S(1)} %bitcast.39, f32[256,8,16,128]{3,2,1,0:T(8,128)} %bitcast.37), kind=kOutput, calls=%fused_computation | convolution fusion | flops 51539607552 | bytes 33554432 | tf_op jit(solution)/shard_map/dot_general | solution.py:41
  414.0 0.0 all-reduce.2.cloned.1.call-update
  414.0 0.0 copy-start.1
  414.0 39.0 %all-reduce.2.cloned.1.call-done = f32[1024,2048]{1,0:T(8,128)} async-done(((f32[1024,2048]{1,0:T(8,128)}), f32[1024,2048]{1,0:T(8,128)}) %all-reduce.2.cloned.1.call-update) | async-done | bytes 8388624 | tf_op jit(solution)/shard_map/psum | solution.py:41
  453.1 6.6 %bitcast_subtract_fusion = f32[1,512,2048]{2,1,0:T(8,128)} fusion(f32[1,512,2048]{2,1,0:T(8,128)} %param.11, f32[1024,2048]{1,0:T(8,128)} %all-reduce.2.cloned.1.call-done, s32[]{:T(128)S(6)} %select_n.3), kind=kLoop, calls=%fused_computation.8 | loop fusion | flops 1048576 | bytes 12582916 | tf_op jit(solution)/shard_map/sub | solution.py:43
  (3 shorter events, 0.0 us)
Async XLA Ops:
  6.5 1.6 copy-start
  6.5 159.2 %all-gather.4.cloned.1.call-start = ((), (), s32[]{:S(2)}) async-start(), calls=%async_computation | async-start | bytes 10485760 | tf_op jit(solution)/shard_map/all_gather | solution.py:35
  13.2 152.5 %copy-start.4 = (s32[1,8,1,8]{3,2,1,0:T(1,128)S(1)}, s32[1,8,1,8]{3,2,1,0:T(1,128)}, u32[]{:S(2)}) copy-start(s32[1,8,1,8]{3,2,1,0:T(1,128)} %param.7) | copy-start | bytes 772
  13.2 310.0 %all-gather.6.cloned.1.call-start = ((), (), s32[]{:S(2)}) async-start(), calls=%async_computation.2 | async-start | bytes 20971520 | tf_op jit(solution)/shard_map/all_gather | solution.py:37
  17.9 435.1 %all-reduce.2.cloned.1.call-start = ((), (), s32[]{:S(2)}) async-start(), calls=%async_computation.1 | async-start | bytes 16777216 | tf_op jit(solution)/shard_map/psum | solution.py:41
  183.0 140.2 %copy-start.3 = (s32[1,8,1,16]{3,2,1,0:T(1,128)S(1)}, s32[1,8,1,16]{3,2,1,0:T(1,128)}, u32[]{:S(2)}) copy-start(s32[1,8,1,16]{3,2,1,0:T(1,128)} %param.9) | copy-start | bytes 1540
  323.2 25.9 %copy-start.2 = (f32[128,8,8,256]{3,1,2,0:T(8,128)S(1)}, f32[128,8,8,256]{3,1,2,0:T(8,128)}, u32[]{:S(2)}) copy-start(f32[128,8,8,256]{3,1,2,0:T(8,128)} %copy.19) | copy-start | bytes 25165828
  414.0 45.6 %copy-start.1 = (f32[1,8,256,256]{3,2,1,0:T(8,128)S(1)}, f32[1,8,256,256]{3,2,1,0:T(8,128)}, u32[]{:S(2)}) copy-start(f32[1,8,256,256]{3,2,1,0:T(8,128)} %param.10) | copy-start | bytes 6291460
Sparse Core Ops, SparseCore 0:
  13.3 152.3 all-gather.3
  167.5 155.6 all-gather.5
  414.2 38.8 all-reduce.1
where the time goes:
time: 472 us; the launch traced here: 466 us
  waiting for transfers between devices  320 us (68%)
  matrix products  108 us (23%)
  local copies, waits for them, and re-layouts  18.4 us (4%)
  between operations  13.4 us (3%)
  other arithmetic  6.56 us (1%)
    all_gather x1, waiting for transfers between devices, body(): lax.all_gather(scaled, 'col', axis=1, tiled=True)  148 us
    all_gather x1, waiting for transfers between devices, body(): lax.all_gather(u_blocks, 'row', axis=1, tiled=True)  133 us
    dot_general x1, matrix products, body(): summed = lax.psum(jnp.dot(l_matrix, u_matrix, precision=highest), 'gz')  64.9 us
    psum x1, waiting for transfers between devices, body(): summed = lax.psum(jnp.dot(l_matrix, u_matrix, precision=highest), 'gz')  39 us
    dot_general x1, matrix products, place_columns(): return jnp.einsum('sak,skwb->swab', onehot, blocks, precision=highest)  25.9 us
    unnamed x12, local copies, waits for them, and re-layouts  13.6 us
    dot_general x1, matrix products, place_rows(): return jnp.einsum('sak,skbw->absw', onehot, blocks, precision=highest)  12.5 us
  transfers between devices with their start and end apart: 3, of which 3 were waited for; matrix products, arithmetic and copies ran while one was open for 6% of the time, Pallas kernels for 0%

commit v1 on v0

--- a/solution.py
+++ b/solution.py
@@ -38,7 +38,7 @@
     l_matrix = l_placed.reshape(AR * B, supernodes * W)
     u_matrix = u_placed.reshape(supernodes * W, AC * B)
     half_rows = ancestor.shape[1]
-    summed = lax.psum(jnp.dot(l_matrix, u_matrix, precision=highest), "gz")
+    summed = jnp.sum(lax.all_gather(jnp.dot(l_matrix, u_matrix, precision=highest), "gz"), axis=0)
     own_share = lax.dynamic_slice_in_dim(summed, lax.axis_index("gz") * half_rows, half_rows, 0)
     return ancestor - own_share[None]
 

time: 472 us -> 476 us (level)
  other arithmetic: 6.56 us -> 18.3 us
  waiting for transfers between devices: 320 us -> 311 us
    psum x1 -> x0, waiting for transfers between devices: 39 us -> none  [body(): summed = lax.psum(jnp.dot(l_matrix, u_matrix, precision=highest), 'gz')]
    all_gather x0 -> x1, waiting for transfers between devices: none -> 30.2 us  [body(): lax.all_gather(jnp.dot(l_matrix, u_matrix, precision=highest), 'gz')]
    reduce_sum x0 -> x1, other arithmetic: none -> 11.8 us  [body(): jnp.sum(lax.all_gather(jnp.dot(l_matrix, u_matrix, precision=highest), 'g...]
where the time goes in v1:
time: 476 us; the launch traced here: 470 us
  waiting for transfers between devices  311 us (65%)
  matrix products  108 us (23%)
  local copies, waits for them, and re-layouts  18.4 us (4%)
  other arithmetic  18.3 us (4%)
  between operations  13.3 us (3%)
    all_gather x1, waiting for transfers between devices, body(): lax.all_gather(scaled, 'col', axis=1, tiled=True)  148 us
    all_gather x1, waiting for transfers between devices, body(): lax.all_gather(u_blocks, 'row', axis=1, tiled=True)  133 us
    dot_general x1, matrix products, body(): jnp.dot(l_matrix, u_matrix, precision=highest)  65.2 us
    all_gather x1, waiting for transfers between devices, body(): lax.all_gather(jnp.dot(l_matrix, u_matrix, precision=highest), 'gz')  30.2 us
    dot_general x1, matrix products, place_columns(): return jnp.einsum('sak,skwb->swab', onehot, blocks, precision=highest)  26 us
    unnamed x12, local copies, waits for them, and re-layouts  13.6 us
    dot_general x1, matrix products, place_rows(): return jnp.einsum('sak,skbw->absw', onehot, blocks, precision=highest)  12.2 us
    reduce_sum x1, other arithmetic, body(): jnp.sum(lax.all_gather(jnp.dot(l_matrix, u_matrix, precision=highest), 'g...  11.8 us
  transfers between devices with their start and end apart: 3, of which 3 were waited for; matrix products, arithmetic and copies ran while one was open for 6% of the time, Pallas kernels for 0%

profile of v1, /device:TPU:0, one launch (start us, length us, event | category | flops | bytes accessed | tf_op | source)
XLA Modules:
  0.0 469.7 jit_solution(5490870169385272396)
XLA Ops:
  6.5 0.0 copy-start
  6.5 0.0 all-gather.6.cloned.1.call-start
  6.5 1.6 copy-done
  8.1 5.1 %fusion.11 = f32[8,2,128,256]{3,2,0,1:T(8,128)} fusion(f32[1,8,256,256]{3,2,1,0:T(8,128)S(1)} %copy-done, f32[1,8,1,2,128,256]{5,4,3,2,1,0:T(8,128)} %param.6), kind=kOutput, calls=%fused_computation.10 | convolution fusion | flops 1610612736 | bytes 6291456 | tf_op jit(solution)/shard_map/skbw,swv->skbv/dot_general | solution.py:29
  13.2 0.0 all-gather.6.cloned.1.call-update
  13.2 0.0 all-gather.8.cloned.1.call-start
  13.3 4.7 copy.13
  17.9 0.0 all-gather.8.cloned.1.call-update
  17.9 0.0 all-gather.10.cloned.1.call-start
  18.0 147.7 %all-gather.6.cloned.1.call-done = f32[8,8,128,256]{3,2,0,1:T(8,128)} async-done(((f32[8,2,128,256]{3,2,0,1:T(8,128)}), f32[8,8,128,256]{3,2,0,1:T(8,128)}) %all-gather.6.cloned.1.call-update) | async-done | bytes 8388624 | tf_op jit(solution)/shard_map/all_gather | solution.py:35
  165.7 0.0 copy-done.4
  165.7 12.2 %fusion.8 = f32[8,128,8,256]{3,0,1,2:T(8,128)S(1)} fusion(f32[8,8,128,256]{3,2,0,1:T(8,128)} %all-gather.6.cloned.1.call-done, s32[8,8]{1,0:T(8,128)S(1)} %bitcast.43), kind=kOutput, calls=%fused_computation.9 | convolution fusion | flops 201327104 | bytes 16777472 | tf_op jit(solution)/shard_map/sak,skbw->absw/dot_general | solution.py:17
  177.9 4.9 %copy.12 = f32[8,128,8,256]{3,2,1,0:T(8,128)S(1)} copy(f32[8,128,8,256]{3,0,1,2:T(8,128)S(1)} %fusion.8) | data formatting | bytes 16777216 | tf_op jit(solution)/shard_map/sak,skbw->absw/transpose | solution.py:17
  182.7 0.0 copy-start.3
  182.7 7.3 %copy.19 = f32[128,8,8,256]{3,1,2,0:T(8,128)} copy(f32[128,8,8,256]{3,2,1,0:T(8,128)S(1)} %bitcast.39) | data formatting | bytes 16777216
  190.1 133.2 %all-gather.8.cloned.1.call-done = f32[1,8,1,16,256,128]{5,4,2,1,0,3:T(8,128)} async-done(((f32[1,8,1,4,256,128]{5,4,2,1,0,3:T(8,128)}), f32[1,8,1,16,256,128]{5,4,2,1,0,3:T(8,128)}) %all-gather.8.cloned.1.call-update) | async-done | bytes 16777232 | tf_op jit(solution)/shard_map/all_gather | solution.py:37
  323.2 0.0 copy-done.3
  323.2 26.0 %fusion.3 = f32[8,16,256,128]{3,1,2,0:T(8,128)} fusion(f32[1,8,1,16,256,128]{5,4,2,1,0,3:T(8,128)} %all-gather.8.cloned.1.call-done, s32[8,16]{1,0:T(8,128)S(1)} %bitcast.42), kind=kOutput, calls=%fused_computation.3 | convolution fusion | flops 805308416 | bytes 33554944 | tf_op jit(solution)/shard_map/sak,skwb->swab/dot_general | solution.py:24
  349.2 0.0 copy-done.2
  349.2 65.2 %fusion = f32[1024,2048]{1,0:T(8,128)} fusion(f32[1024,2048]{1,0:T(8,128)S(1)} %bitcast.41, f32[256,8,16,128]{3,2,1,0:T(8,128)} %bitcast.38), kind=kOutput, calls=%fused_computation | convolution fusion | flops 51539607552 | bytes 33554432 | tf_op jit(solution)/shard_map/dot_general | solution.py:41
  414.4 0.0 all-gather.10.cloned.1.call-update
  414.4 30.2 %all-gather.10.cloned.1.call-done = f32[2048,2048]{1,0:T(8,128)} async-done(((f32[1024,2048]{1,0:T(8,128)}), f32[2048,2048]{1,0:T(8,128)}) %all-gather.10.cloned.1.call-update) | async-done | bytes 16777232 | tf_op jit(solution)/shard_map/all_gather | solution.py:41
  444.7 11.8 %reduce_sum.9 = f32[1024,2048]{1,0:T(8,128)} reduce(f32[2,1024,2048]{2,1,0:T(8,128)} %bitcast.40, f32[]{:T(128)} %constant.2.clone.1), dimensions={0}, to_apply=%region_0.0 | reduce | flops 2097152 | bytes 25165828 | tf_op jit(solution)/shard_map/reduce_sum | solution.py:41
  456.4 6.6 %bitcast_subtract_fusion = f32[1,512,2048]{2,1,0:T(8,128)} fusion(f32[1,512,2048]{2,1,0:T(8,128)} %param.11, f32[1024,2048]{1,0:T(8,128)} %reduce_sum.9, s32[]{:T(128)S(6)} %select_n.3), kind=kLoop, calls=%fused_computation.8 | loop fusion | flops 1048576 | bytes 12582916 | tf_op jit(solution)/shard_map/sub | solution.py:43
  (4 shorter events, 0.0 us)
Async XLA Ops:
  6.5 1.6 copy-start
  6.5 159.2 %all-gather.6.cloned.1.call-start = ((), (), s32[]{:S(2)}) async-start(), calls=%async_computation | async-start | bytes 10485760 | tf_op jit(solution)/shard_map/all_gather | solution.py:35
  13.2 152.5 %copy-start.4 = (s32[1,8,1,8]{3,2,1,0:T(1,128)S(1)}, s32[1,8,1,8]{3,2,1,0:T(1,128)}, u32[]{:S(2)}) copy-start(s32[1,8,1,8]{3,2,1,0:T(1,128)} %param.7) | copy-start | bytes 772
  13.2 310.0 %all-gather.8.cloned.1.call-start = ((), (), s32[]{:S(2)}) async-start(), calls=%async_computation.1 | async-start | bytes 20971520 | tf_op jit(solution)/shard_map/all_gather | solution.py:37
  17.9 426.7 %all-gather.10.cloned.1.call-start = ((), (), s32[]{:S(2)}) async-start(), calls=%async_computation.2 | async-start | bytes 25165824 | tf_op jit(solution)/shard_map/all_gather | solution.py:41
  182.7 140.5 %copy-start.3 = (s32[1,8,1,16]{3,2,1,0:T(1,128)S(1)}, s32[1,8,1,16]{3,2,1,0:T(1,128)}, u32[]{:S(2)}) copy-start(s32[1,8,1,16]{3,2,1,0:T(1,128)} %param.9) | copy-start | bytes 1540
  323.2 26.0 %copy-start.2 = (f32[128,8,8,256]{3,1,2,0:T(8,128)S(1)}, f32[128,8,8,256]{3,1,2,0:T(8,128)}, u32[]{:S(2)}) copy-start(f32[128,8,8,256]{3,1,2,0:T(8,128)} %copy.19) | copy-start | bytes 25165828
  444.7 18.3 %copy-start.1 = (f32[1,8,256,256]{3,2,1,0:T(8,128)S(1)}, f32[1,8,256,256]{3,2,1,0:T(8,128)}, u32[]{:S(2)}) copy-start(f32[1,8,256,256]{3,2,1,0:T(8,128)} %param.10) | copy-start | bytes 6291460
Sparse Core Ops, SparseCore 0:
  13.3 152.3 all-gather.5
  167.5 155.6 all-gather.7
  414.5 30.0 all-gather.9
